TPU v7x, 32 devices: a whole 2x2x4 slice. The times are simulated.
32 devices in a mesh: clu: 8 (over z, y), grp: 4 (over x, core).
Axes of the slice: x: 2, y: 2, z: 4, core: 2. Of those that a mesh axis runs over, the one named last changes fastest.
Arguments:
- embeddings: bfloat16 [16384, 768], P(('clu', 'grp')), may hold values from -6 to 6
- cluster_of: int32 [16384], P(('clu', 'grp')), may hold values from 0 to 15, as said below
- new_rows: bfloat16 [512, 768], P(('clu', 'grp')), may hold values from -6 to 6
- centroids: bfloat16 [8192, 768], P(('clu', 'grp')), may hold values from -6 to 6
Outputs:
- dup_score: float32 [16384], P(('clu', 'grp'))
- centroid_score: float32 [512], P(('clu', 'grp'))
Inputs may be any that keep to these rules, and one draw needn't show every extreme that they name: `cluster_of`: cluster k is owned by owner k mod 8; among the 512 rows of one device, at most 128 rows belong to the clusters of one owner, and in every such block some owner has exactly 128.
All inputs are finite; a program needn't handle non-finite values.
Results may differ from a plain program's by a relative error of at most 0.0015.
Values may be sent and summed in bfloat16 or wider, within the bound.
A program may use at most 64 MiB of HBM per device.

v0:
```python
import jax
import jax.numpy as jnp
from jax import lax
from jax.sharding import PartitionSpec as P

epsilon = 1e-06


def normalize(values):
    wide = values.astype(jnp.float32)
    total = jnp.sum(wide * wide, axis=-1, keepdims=True)
    return (wide * lax.rsqrt(total + epsilon)).astype(jnp.bfloat16)


def pair_scores(left_units, right_units):
    return lax.dot_general(
        left_units, right_units, (((1,), (1,)), ((), ())), preferred_element_type=jnp.float32
    )


def best_over(cent_units, incoming):
    return jnp.max(pair_scores(incoming, cent_units), axis=1)


def shards(embeddings, cluster_of, new_rows, centroids):
    clu_count = lax.axis_size("clu")
    row_count = embeddings.shape[0]
    width = embeddings.shape[1]
    slot_cap = 2 * row_count // clu_count
    slot_total = clu_count * slot_cap
    normed = normalize(embeddings)
    target = cluster_of % clu_count
    target_hot = (target[:, None] == jnp.arange(clu_count, dtype=jnp.int32)[None, :]).astype(
        jnp.float32
    )
    earlier = (jnp.arange(row_count)[:, None] > jnp.arange(row_count)[None, :]).astype(jnp.float32)
    preceding = jnp.dot(earlier, target_hot, preferred_element_type=jnp.float32)
    row_rank = jnp.sum(preceding * target_hot, axis=1).astype(jnp.int32)
    row_slot = target * slot_cap + row_rank
    send_units = (
        jnp.zeros((slot_total, width), jnp.bfloat16)
        .at[row_slot]
        .set(normed)
        .reshape(clu_count, slot_cap, width)
    )
    cluster_value = cluster_of.astype(jnp.float32).astype(jnp.bfloat16)
    send_ids = (
        jnp.full((slot_total,), -1.0, jnp.bfloat16)
        .at[row_slot]
        .set(cluster_value)
        .reshape(clu_count, slot_cap)
    )
    recv_units, recv_ids = (
        lax.all_to_all(send_units, "clu", split_axis=0, concat_axis=0, tiled=True),
        lax.all_to_all(send_ids, "clu", split_axis=0, concat_axis=0, tiled=True),
    )
    members = recv_units.reshape(slot_total, width)
    member_ids = recv_ids.reshape(slot_total)
    valid_own = member_ids >= 0
    grp_index = lax.axis_index("grp")
    own_pos = grp_index * slot_total + jnp.arange(slot_total, dtype=jnp.int32)
    other_units = lax.all_gather(members, "grp", axis=0, tiled=True)
    other_ids = lax.all_gather(member_ids, "grp", axis=0, tiled=True)
    piece_rows = other_units.shape[0]
    scores = pair_scores(members, other_units)
    matched = (member_ids[:, None] == other_ids[None, :]) & valid_own[:, None]
    scores, matched = (scores, matched)
    other_pos = jnp.arange(piece_rows, dtype=jnp.int32)
    matched = matched & (own_pos[:, None] != other_pos[None, :])
    best_match = jnp.maximum(
        jnp.full((slot_total,), -1.0, jnp.float32),
        jnp.max(jnp.where(matched, scores, -1.0), axis=1),
    )
    returned_best = lax.all_to_all(
        best_match.reshape(clu_count, slot_cap), "clu", split_axis=0, concat_axis=0, tiled=True
    ).reshape(slot_total)
    dup_score = returned_best[row_slot]
    new_unit = normalize(new_rows)
    cent_unit = normalize(centroids)
    cent_group = lax.all_gather(cent_unit, "grp", axis=0, tiled=True)
    partial_best = best_over(cent_group, lax.all_gather(new_unit, "clu", axis=0, tiled=True))
    overall = lax.pmax(partial_best, "clu")
    own_start = lax.axis_index("clu") * new_unit.shape[0]
    centroid_score = lax.dynamic_slice_in_dim(overall, own_start, new_unit.shape[0])
    return (dup_score, centroid_score)


def solution(mesh):
    return jax.shard_map(
        shards,
        mesh=mesh,
        in_specs=(
            P(("clu", "grp"), None),
            P(("clu", "grp")),
            P(("clu", "grp"), None),
            P(("clu", "grp"), None),
        ),
        out_specs=(P(("clu", "grp")), P(("clu", "grp"))),
        check_vma=False,
    )
```

profile of v0, /device:TPU:0, one launch (start us, length us, event | category | flops | bytes accessed | tf_op | source)
XLA Modules:
  0.0 158.8 jit_solution(16503514977000376426)
XLA Ops:
  7.2 0.0 copy-start.1
  7.2 0.0 all-gather.3.cloned.1.call-start
  7.2 0.8 add_select_fusion
  8.0 0.3 fusion.3
  8.2 0.8 convert_convert_fusion
  9.0 1.4 fusion.1
  10.4 0.0 copy-done.1
  10.4 3.1 %scatter_custom_fusion.1 = bf16[1024,768]{1,0:T(8,128)(2,1)S(1)} fusion(s32[512]{0:T(512)S(1)} %get-tuple-element.3, bf16[512,768]{1,0:T(8,128)(2,1)S(1)} %copy-done.1, f32[512]{0:T(512)S(1)} %add_rsqrt_fusion, bf16[]{:T(256)} %constant.22.clone.1), kind=kCustom, calls=%fused_computation.18 | custom fusion | flops 1179648 | bytes 2361346 | tf_op jit(solution)/shard_map/scatter | solution.py:43
  13.5 44.2 %all_to_all.20 = bf16[8,128,768]{2,1,0:T(8,128)(2,1)} all-to-all(bf16[8,128,768]{2,1,0:T(8,128)(2,1)S(1)} %bitcast.14), channel_id=1, replica_groups=mesh['clu'=8,'grp'=4] {'clu'}, dimensions={0} | all-to-all | bytes 3145728 | tf_op jit(solution)/shard_map/all_to_all | solution.py:54
  57.7 0.0 copy-start.2
  57.7 0.0 copy-start.3
  57.7 0.0 copy-start
  57.7 0.0 all-gather.3.cloned.1.call-update
  57.7 3.8 %scatter_custom_fusion = bf16[1024]{0:T(1024)(128)(2,1)S(1)} fusion(s32[512]{0:T(512)S(1)} %get-tuple-element.3, bf16[512]{0:T(512)(128)(2,1)S(1)} %get-tuple-element.2, bf16[]{:T(256)} %constant.15.clone.1), kind=kCustom, calls=%fused_computation.39 | custom fusion | bytes 2050 | tf_op jit(solution)/shard_map/scatter | solution.py:50
  61.5 0.6 copy.6
  62.1 3.6 %all-to-all-start = ((bf16[8,1,128]{2,1,0:T(2,128)(2,1)}), bf16[8,1,128]{2,1,0:T(2,128)(2,1)S(1)}, u32[]{:S(2)}, u32[]{:S(2)}) async-start(bf16[8,1,128]{2,1,0:T(2,128)(2,1)} %copy.6), calls=%async_computation | async-start | bytes 8192 | tf_op jit(solution)/shard_map/all_to_all | solution.py:55
  65.7 0.0 all-gather.5.cloned.1.call-start
  65.8 0.0 copy-done.2
  65.8 0.2 fusion.4
  65.9 0.9 fusion.5
  66.8 0.0 all-gather.5.cloned.1.call-update
  66.9 0.0 copy-done.3
  66.9 0.1 fusion.10
  67.0 0.1 fusion.11
  67.1 31.3 %all_gather.14 = bf16[128,768]{1,0:T(8,128)(2,1)S(1)} all-gather(bf16[16,768]{1,0:T(8,128)(2,1)S(1)} %fusion.11), channel_id=1, replica_groups=mesh['clu'=8,'grp'=4] {'clu'}, dimensions={0}, use_global_device_ids=true | all-gather | bytes 221184 | tf_op jit(solution)/shard_map/all_gather | solution.py:81
  98.4 0.0 all-to-all-done
  98.4 5.2 %all_gather.12 = bf16[4096]{0:T(1024)(128)(2,1)S(1)} all-gather(bf16[1024]{0:T(1024)(128)(2,1)S(1)} %bitcast.15), channel_id=1, replica_groups=mesh['clu'=8,'grp'=4] {'grp'}, dimensions={0}, use_global_device_ids=true | all-gather | bytes 10240 | tf_op jit(solution)/shard_map/all_gather | solution.py:63
  103.6 0.0 all-gather.3.cloned.1.call-done
  103.6 0.0 copy-done
  103.6 11.5 %select_reduce_fusion = f32[1024]{0:T(1024)S(1)} fusion(s32[1024]{0:T(1024)S(1)} %iota_add_fusion, pred[1024]{0:T(1024)(128)(4,1)S(1)} %broadcast_compare_fusion, bf16[1024,768]{1,0:T(8,128)(2,1)S(1)} %bitcast.13, bf16[4096,768]{1,0:T(8,128)(2,1)} %all-gather.3.cloned.1.call-done, bf16[4096]{0:T(1024)(128)(2,1)S(1)} %all_gather.12, ...), kind=kOutput, calls=%fused_computation.3 | convolution fusion | flops 6476004352 | bytes 7883776 | tf_op jit(solution)/shard_map/dot_general | solution.py:16
  115.1 0.6 broadcast_maximum_fusion
  115.7 5.3 %all-to-all-start.2 = ((f32[8,1,128]{2,1,0:T(1,128)}), f32[8,1,128]{2,1,0:T(1,128)S(1)}, u32[]{:S(2)}, u32[]{:S(2)}) async-start(f32[8,1,128]{2,1,0:T(1,128)} %bitcast.3), calls=%async_computation.2 | async-start | bytes 8192 | tf_op jit(solution)/shard_map/all_to_all | solution.py:74
  121.0 3.5 %all-gather.5.cloned.1.call-done = bf16[1024,768]{1,0:T(8,128)(2,1)} async-done(((bf16[256,768]{1,0:T(8,128)(2,1)}), bf16[1024,768]{1,0:T(8,128)(2,1)}) %all-gather.5.cloned.1.call-update) | async-done | bytes 1572880 | tf_op jit(solution)/shard_map/all_gather | solution.py:80
  124.5 2.1 %convolution_reduce_fusion = f32[128]{0:T(128)S(1)} fusion(bf16[128,768]{1,0:T(8,128)(2,1)S(1)} %all_gather.14, bf16[1024,768]{1,0:T(8,128)(2,1)} %all-gather.5.cloned.1.call-done), kind=kOutput, calls=%fused_computation.10 | convolution fusion | flops 201457536 | bytes 1769984 | tf_op jit(solution)/shard_map/dot_general | solution.py:16
  126.6 21.4 %pmax.7 = f32[128]{0:T(128)S(1)} all-reduce(f32[128]{0:T(128)S(1)} %convolution_reduce_fusion), channel_id=1, replica_groups=mesh['clu'=8,'grp'=4] {'clu'}, use_global_device_ids=true, to_apply=%region_8.9 | all-reduce | flops 128 | bytes 1024 | tf_op jit(solution)/shard_map/pmax | solution.py:82
  148.0 0.6 dynamic_slice.3
  148.6 0.0 all-to-all-done.2
  148.6 3.4 %gather_fusion = f32[512]{0:T(512)} fusion(f32[1024]{0:T(1024)S(1)} %bitcast.11, s32[1024]{0:T(1024)S(1)} %pad_clamp_fusion), kind=kCustom, calls=%fused_computation | custom fusion | bytes 6144 | tf_op jit(solution)/shard_map/gather | solution.py:77
  (7 shorter events, 0.1 us)
Async XLA Ops:
  7.2 3.2 %copy-start.1 = (bf16[512,768]{1,0:T(8,128)(2,1)S(1)}, bf16[512,768]{1,0:T(8,128)(2,1)}, u32[]{:S(2)}) copy-start(bf16[512,768]{1,0:T(8,128)(2,1)} %param.4) | copy-start | bytes 2359300
  7.2 96.4 %all-gather.3.cloned.1.call-start = ((), (), s32[]{:S(2)}) async-start(), calls=%async_computation.3 | async-start | bytes 7864320 | tf_op jit(solution)/shard_map/all_gather | solution.py:62
  57.7 8.0 %copy-start.2 = (bf16[256,768]{1,0:T(8,128)(2,1)S(1)}, bf16[256,768]{1,0:T(8,128)(2,1)}, u32[]{:S(2)}) copy-start(bf16[256,768]{1,0:T(8,128)(2,1)} %param.7) | copy-start | bytes 1179652
  57.7 9.2 %copy-start.3 = (bf16[16,768]{1,0:T(8,128)(2,1)S(1)}, bf16[16,768]{1,0:T(8,128)(2,1)}, u32[]{:S(2)}) copy-start(bf16[16,768]{1,0:T(8,128)(2,1)} %param.6) | copy-start | bytes 73732
  57.7 45.9 %copy-start = (bf16[8,128,768]{2,1,0:T(8,128)(2,1)S(1)}, bf16[8,128,768]{2,1,0:T(8,128)(2,1)}, u32[]{:S(2)}) copy-start(bf16[8,128,768]{2,1,0:T(8,128)(2,1)} %all_to_all.20) | copy-start | bytes 4718596
  62.1 36.2 %all-to-all-start = ((bf16[8,1,128]{2,1,0:T(2,128)(2,1)}), bf16[8,1,128]{2,1,0:T(2,128)(2,1)S(1)}, u32[]{:S(2)}, u32[]{:S(2)}) async-start(bf16[8,1,128]{2,1,0:T(2,128)(2,1)} %copy.6), calls=%async_computation | async-start | bytes 8192 | tf_op jit(solution)/shard_map/all_to_all | solution.py:55
  65.7 58.8 %all-gather.5.cloned.1.call-start = ((), (), s32[]{:S(2)}) async-start(), calls=%async_computation.4 | async-start | bytes 1966080 | tf_op jit(solution)/shard_map/all_gather | solution.py:80
  115.7 32.8 %all-to-all-start.2 = ((f32[8,1,128]{2,1,0:T(1,128)}), f32[8,1,128]{2,1,0:T(1,128)S(1)}, u32[]{:S(2)}, u32[]{:S(2)}) async-start(f32[8,1,128]{2,1,0:T(1,128)} %bitcast.3), calls=%async_computation.2 | async-start | bytes 8192 | tf_op jit(solution)/shard_map/all_to_all | solution.py:74
Sparse Core Ops, SparseCore 0:
  57.9 45.3 all-gather.2
  104.8 19.6 all-gather.4
where the time goes:
time: 159 us
  blocking collectives  102 us (64%)
  between operations  14.1 us (9%)
  matrix products  13.9 us (9%)
  starting transfers between devices  8.96 us (6%)
  local copies, waits for them, and re-layouts  8.38 us (5%)
  other arithmetic  7.88 us (5%)
  waiting for transfers between devices  3.5 us (2%)
    all_to_all x1, blocking collectives, shards(): lax.all_to_all(send_units, 'clu', split_axis=0, concat_axis=0, tiled=True)  44.2 us
    all_gather x1, blocking collectives, shards(): lax.all_gather(new_unit, 'clu', axis=0, tiled=True)  31.3 us
    pmax x1, blocking collectives, shards(): overall = lax.pmax(partial_best, 'clu')  21.4 us
    dot_general x2, matrix products, pair_scores(): lax.dot_general(left_units, right_units, (((1,), (1,)), ((), ())), prefer...  13.7 us
    all_to_all x1, starting transfers between devices, shards(): lax.all_to_all(best_match.reshape(clu_count, slot_cap), 'clu', split_axis...  5.3 us
    all_gather x1, blocking collectives, shards(): other_ids = lax.all_gather(member_ids, 'grp', axis=0, tiled=True)  5.19 us
    scatter x1, local copies, waits for them, and re-layouts, shards(): send_ids = jnp.full((slot_total,), -1.0, jnp.bfloat16).at[row_slot].set(c...  3.77 us
    all_to_all x1, starting transfers between devices, shards(): lax.all_to_all(send_ids, 'clu', split_axis=0, concat_axis=0, tiled=True)  3.59 us
  transfers between devices with their start and end apart: 4, of which 1 were waited for; matrix products, arithmetic and copies ran while one was open for 13% of the time, Pallas kernels for 0%

commit v1 on v0

v1 whole, which is shorter than its diff:
```python
import functools

import jax
import jax.numpy as jnp
from jax import lax
from jax.experimental import pallas as pl
from jax.experimental.pallas import tpu as pltpu
from jax.sharding import PartitionSpec as P

epsilon = 1e-06
lanes = 128
chunk_order = (0, 1, 6, 7, 2, 3, 4, 5)
chunk_count = len(chunk_order)
stage_count = chunk_count // 2
MESH = pl.DeviceIdType.MESH


def normalize(values):
    wide = values.astype(jnp.float32)
    total = jnp.sum(wide * wide, axis=-1, keepdims=True)
    return (wide * lax.rsqrt(total + epsilon)).astype(jnp.bfloat16)


def pair_scores(left_units, right_units):
    return lax.dot_general(
        left_units, right_units, (((1,), (1,)), ((), ())), preferred_element_type=jnp.float32
    )


def pack_kernel(clu_count, cap, emb_ref, cluster_ref, new_ref, send_ref, ids_ref, slot_ref, unit_ref):
    per_chunk = clu_count // chunk_count
    rows = emb_ref.shape[0]
    slots = clu_count * cap
    me = lax.axis_index("clu")
    unit_ref[...] = normalize(new_ref[...])
    cluster = cluster_ref[...]
    distance = (cluster & (clu_count - 1)) ^ me
    far_chunk = distance // per_chunk
    place = jnp.zeros_like(distance)
    for position, chunk in enumerate(chunk_order):
        place = jnp.where(far_chunk == chunk, position, place)
    place = place * per_chunk + distance % per_chunk
    owner_hot = lax.broadcasted_iota(jnp.int32, (clu_count, rows), 0) == place
    before = lax.broadcasted_iota(jnp.int32, (rows, rows), 0) < lax.broadcasted_iota(
        jnp.int32, (rows, rows), 1
    )
    preceding = jnp.dot(
        owner_hot.astype(jnp.bfloat16),
        before.astype(jnp.bfloat16),
        preferred_element_type=jnp.float32,
    )
    rank = jnp.sum(jnp.where(owner_hot, preceding, 0.0), axis=0, keepdims=True).astype(jnp.int32)
    slot = place * cap + rank
    slot_ref[...] = slot
    chosen = (lax.broadcasted_iota(jnp.int32, (slots, rows), 0) == slot).astype(jnp.bfloat16)
    units = normalize(emb_ref[...])
    send_ref[...] = jnp.dot(chosen, units, preferred_element_type=jnp.float32).astype(jnp.bfloat16)
    marks = jnp.broadcast_to((cluster + 1).astype(jnp.float32), (8, rows)).astype(jnp.bfloat16)
    slot_marks = pair_scores(marks, chosen)
    lane_block = lax.broadcasted_iota(jnp.int32, (8, lanes), 1) // cap
    for block in range(clu_count):
        chunk, inner = divmod(block, per_chunk)
        tile = slot_marks[:, chunk * lanes : (chunk + 1) * lanes]
        ids_ref[block] = jnp.where(lane_block == inner, tile, 0.0)


def exchange_kernel(
    clu_count,
    cap,
    new_count,
    send_ref,
    ids_ref,
    slot_ref,
    new_ref,
    cent_ref,
    dup_ref,
    best_ref,
    held,
    held_ids,
    marks,
    id_rows,
    own_acc,
    mate_acc,
    mate_in,
    new_held,
    cent_unit,
    part,
    part_in,
    message,
    message_in,
    local_sem,
    data_send,
    data_recv,
    id_send,
    id_recv,
    new_send,
    new_recv,
    fwd_send,
    fwd_recv,
    fwd_id_send,
    fwd_id_recv,
    wide_send,
    wide_recv,
    part_send,
    part_recv,
    mate_send,
    mate_recv,
    msg_send,
    msg_recv,
):
    per_chunk = clu_count // chunk_count
    half = lanes
    stage_rows = 2 * half
    me = lax.axis_index("clu")
    grp = lax.axis_index("grp")

    def far(block):
        chunk, inner = divmod(block, per_chunk)
        return {"clu": me ^ (chunk_order[chunk] * per_chunk + inner), "grp": grp}

    def near(step):
        return {"clu": me, "grp": grp ^ step}

    def chunk_row(chunk, kind):
        stage, part_of = divmod(chunk, 2)
        return stage * 3 * stage_rows + kind * stage_rows + part_of * half

    def block_rows(block):
        chunk, inner = divmod(block, per_chunk)
        return pl.ds(chunk_row(chunk, 0) + inner * cap, cap)

    def remote(src, dst, send_sem, recv_sem, device):
        return pltpu.make_async_remote_copy(
            src_ref=src,
            dst_ref=dst,
            send_sem=send_sem,
            recv_sem=recv_sem,
            device_id=device,
            device_id_type=MESH,
        )

    barrier = pltpu.get_barrier_semaphore()
    for block in range(1, clu_count):
        pl.semaphore_signal(barrier, inc=1, device_id=far(block), device_id_type=MESH)
    for step in (1, 2, 3):
        pl.semaphore_signal(barrier, inc=1, device_id=near(step), device_id_type=MESH)

    local = [
        pltpu.make_async_copy(send_ref.at[pl.ds(0, cap)], held.at[block_rows(0)], local_sem.at[0]),
        pltpu.make_async_copy(ids_ref.at[0], held_ids.at[0, 0], local_sem.at[1]),
        pltpu.make_async_copy(new_ref, new_held.at[0, pl.ds(0, new_count)], local_sem.at[2]),
    ]
    for copy in local:
        copy.start()
    pl.semaphore_wait(barrier, clu_count - 1 + 3)

    new_copies = []
    data_copies = [None]
    id_copies = [None]
    for block in range(1, clu_count):
        new_copies.append(
            remote(
                new_ref,
                new_held.at[0, pl.ds(block * new_count, new_count)],
                new_send.at[block],
                new_recv.at[block],
                far(block),
            )
        )
        id_copies.append(
            remote(
                ids_ref.at[block],
                held_ids.at[0, block],
                id_send.at[block],
                id_recv.at[block],
                far(block),
            )
        )
        data_copies.append(
            remote(
                send_ref.at[pl.ds(block * cap, cap)],
                held.at[block_rows(block)],
                data_send.at[block],
                data_recv.at[block],
                far(block),
            )
        )
    for copy in new_copies:
        copy.start()
    for block in range(1, clu_count):
        id_copies[block].start()
        data_copies[block].start()

    own_acc[...] = jnp.full(own_acc.shape, -1.0, jnp.float32)
    mate_acc[...] = jnp.full(mate_acc.shape, -1.0, jnp.float32)
    cent_unit[...] = normalize(cent_ref[...])

    forwards = {}

    def spread_marks(chunk, kind):
        tile = held_ids[kind, chunk * per_chunk]
        for inner in range(1, per_chunk):
            tile = tile + held_ids[kind, chunk * per_chunk + inner]
        square = jnp.concatenate([tile] * (lanes // 8), axis=0)
        marks[pl.ds(chunk_row(chunk, kind), half), :] = jnp.transpose(square)
        if kind < 2:
            stage, part_of = divmod(chunk, 2)
            id_rows[stage, kind, :, pl.ds(part_of * half, half)] = tile

    def pass_on(chunk):
        for inner in range(per_chunk):
            block = chunk * per_chunk + inner
            if block == 0:
                local[0].wait()
                local[1].wait()
            else:
                id_copies[block].wait_recv()
                data_copies[block].wait_recv()
        src_rows = pl.ds(chunk_row(chunk, 0), half)
        src_ids = pl.ds(chunk * per_chunk, per_chunk)
        for kind in (2, 1):
            index = (kind - 1) * chunk_count + chunk
            ids = remote(
                held_ids.at[0, src_ids],
                held_ids.at[kind, src_ids],
                fwd_id_send.at[index],
                fwd_id_recv.at[index],
                near(kind),
            )
            data = remote(
                held.at[src_rows],
                held.at[pl.ds(chunk_row(chunk, kind), half)],
                fwd_send.at[index],
                fwd_recv.at[index],
                near(kind),
            )
            ids.start()
            data.start()
            forwards[chunk, kind] = (ids, data)
        spread_marks(chunk, 0)

    def receive(chunk):
        for kind in (1, 2):
            ids, data = forwards[chunk, kind]
            ids.wait_recv()
            data.wait_recv()
            spread_marks(chunk, kind)

    def fold(scores, matched):
        kept = jnp.where(matched, scores, -1.0)
        return jnp.max(kept.reshape(stage_rows // 8, 8, stage_rows), axis=0)

    def compute(stage):
        receive(2 * stage)
        receive(2 * stage + 1)

        def body(step, carry):
            left = jnp.minimum(step, stage)
            right = jnp.where(step <= stage, stage, step - stage - 1)
            left_base = left * (3 * stage_rows)
            right_base = right * (3 * stage_rows)
            own_cols = held[pl.ds(pl.multiple_of(right_base, stage_rows), stage_rows), :]
            mate_cols = held[
                pl.ds(pl.multiple_of(right_base + stage_rows, stage_rows), stage_rows), :
            ]
            own_ids = id_rows[right, 0][0:1]
            mate_ids = id_rows[right, 1][0:1]
            best = own_acc[right]
            for kind in range(3):
                rows = pl.ds(
                    pl.multiple_of(left_base + kind * stage_rows, stage_rows), stage_rows
                )
                others = held[rows, :]
                mark = marks[rows, :]
                mark = jnp.concatenate([mark, mark], axis=1)
                matched = mark == own_ids
                if kind == 0:
                    row_id = lax.broadcasted_iota(jnp.int32, (stage_rows, stage_rows), 0)
                    col_id = lax.broadcasted_iota(jnp.int32, (stage_rows, stage_rows), 1)
                    shift = (right - left) * stage_rows
                    matched = matched & (row_id - col_id != shift)
                best = jnp.maximum(best, fold(pair_scores(others, own_cols), matched))
                if kind == 2:
                    mate_acc[right] = jnp.maximum(
                        mate_acc[right],
                        fold(pair_scores(others, mate_cols), mark == mate_ids),
                    )
            own_acc[right] = best
            return carry

        lax.fori_loop(0, 2 * stage + 1, body, 0)

    group_rows = clu_count * new_count
    cross_new = remote(
        new_held.at[0], new_held.at[2], wide_send.at[0], wide_recv.at[0], near(2)
    )
    mate_new = remote(new_held.at[0], new_held.at[1], wide_send.at[1], wide_recv.at[1], near(1))
    corner_new = remote(new_held.at[2], new_held.at[3], wide_send.at[2], wide_recv.at[2], near(1))
    part_copies = [
        remote(
            part.at[step],
            part_in.at[step - 1],
            part_send.at[step - 1],
            part_recv.at[step - 1],
            near(step),
        )
        for step in (1, 2, 3)
    ]

    def new_first():
        local[2].wait()
        for copy in new_copies:
            copy.wait_recv()
        cross_new.start()
        mate_new.start()

    def new_second():
        cross_new.wait_recv()
        corner_new.start()

    def new_third():
        mate_new.wait_recv()
        corner_new.wait_recv()
        for step in range(4):
            scores = pair_scores(cent_unit[...], new_held[step])
            top = jnp.max(
                scores.reshape(scores.shape[0] // 8, 8, group_rows), axis=0
            )
            top = jnp.max(top, axis=0, keepdims=True)
            if group_rows == lanes:
                part[step] = jnp.broadcast_to(top, (8, lanes))
            else:
                for row in range(group_rows // lanes):
                    part[step, row : row + 1, :] = top[:, row * lanes : (row + 1) * lanes]
        for copy in part_copies:
            copy.start()

    pass_on(0)
    pass_on(1)
    new_first()
    pass_on(2)
    new_second()
    pass_on(3)
    new_third()
    compute(0)
    pass_on(4)
    pass_on(5)
    compute(1)
    pass_on(6)
    pass_on(7)
    compute(2)
    compute(3)

    mate_copy = remote(mate_acc, mate_in, mate_send.at[0], mate_recv.at[0], near(1))
    mate_copy.start()
    cent_best = part[0]
    for step in (1, 2, 3):
        part_copies[step - 1].wait_recv()
        cent_best = jnp.maximum(cent_best, part_in[step - 1])
    mate_copy.wait_recv()
    for stage in range(stage_count):
        final = jnp.max(
            jnp.maximum(own_acc[stage], mate_in[stage]), axis=0, keepdims=True
        )
        for part_of in range(2):
            message[2 * stage + part_of, 0:8, :] = jnp.broadcast_to(
                final[:, part_of * half : (part_of + 1) * half], (8, lanes)
            )
            message[2 * stage + part_of, 8:, :] = cent_best
    messages = []
    for block in range(1, clu_count):
        copy = remote(
            message.at[block // per_chunk],
            message_in.at[block],
            msg_send.at[block],
            msg_recv.at[block],
            far(block),
        )
        copy.start()
        messages.append(copy)
    message_in[0] = message[0]
    for block in range(1, clu_count):
        new_copies[block - 1].wait_send()
        id_copies[block].wait_send()
        data_copies[block].wait_send()
    for ids, data in forwards.values():
        ids.wait_send()
        data.wait_send()
    for copy in (cross_new, mate_new, corner_new, mate_copy, *part_copies):
        copy.wait_send()
    for copy in messages:
        copy.wait()

    slot = slot_ref[...]
    lane_block = lax.broadcasted_iota(jnp.int32, (1, lanes), 1) // cap
    row_list = []
    for chunk in range(chunk_count):
        row = message_in[chunk * per_chunk, 0:1, :]
        for inner in range(1, per_chunk):
            row = jnp.where(lane_block == inner, message_in[chunk * per_chunk + inner, 0:1, :], row)
        row_list.append(row)
    columns = jnp.transpose(
        jnp.concatenate([jnp.broadcast_to(row, (16, lanes)) for row in row_list], axis=0)
    )
    total = jnp.zeros(slot.shape, jnp.float32)
    position = lax.broadcasted_iota(jnp.int32, (lanes, slot.shape[1]), 0)
    for chunk in range(chunk_count):
        column = columns[:, chunk * 16 : chunk * 16 + 1]
        total = total + jnp.sum(
            jnp.where(position + chunk * lanes == slot, column, 0.0), axis=0, keepdims=True
        )
    dup_ref[...] = total
    best = None
    for block in range(clu_count):
        start = block * new_count
        row = 8 + start // lanes
        piece = message_in[block, row : row + 1, :][:, start % lanes : start % lanes + new_count]
        best = piece if best is None else jnp.maximum(best, piece)
    best_ref[...] = best


def shards(embeddings, cluster_of, new_rows, centroids):
    clu_count = lax.axis_size("clu")
    rows, width = embeddings.shape
    new_count = new_rows.shape[0]
    cap = 2 * rows // clu_count
    slots = clu_count * cap
    assert slots == chunk_count * lanes
    assert lax.axis_size("grp") == 4
    vmem = pl.BlockSpec(memory_space=pltpu.VMEM)
    anywhere = pl.BlockSpec(memory_space=pl.ANY)
    send_units, send_ids, slot, new_unit = pl.pallas_call(
        functools.partial(pack_kernel, clu_count, cap),
        out_shape=(
            jax.ShapeDtypeStruct((slots, width), jnp.bfloat16),
            jax.ShapeDtypeStruct((clu_count, 8, lanes), jnp.float32),
            jax.ShapeDtypeStruct((1, rows), jnp.int32),
            jax.ShapeDtypeStruct((new_count, width), jnp.bfloat16),
        ),
        in_specs=[vmem] * 3,
        out_specs=(vmem,) * 4,
        name="pack",
    )(embeddings, cluster_of.reshape(1, rows), new_rows)
    dma = pltpu.SemaphoreType.DMA
    group_rows = clu_count * new_count
    stage_rows = 2 * lanes
    dup, best = pl.pallas_call(
        functools.partial(exchange_kernel, clu_count, cap, new_count),
        out_shape=(
            jax.ShapeDtypeStruct((1, rows), jnp.float32),
            jax.ShapeDtypeStruct((1, new_count), jnp.float32),
        ),
        in_specs=[anywhere, anywhere, vmem, anywhere, vmem],
        out_specs=(vmem, vmem),
        scratch_shapes=[
            pltpu.VMEM((3 * slots, width), jnp.bfloat16),
            pltpu.VMEM((3, clu_count, 8, lanes), jnp.float32),
            pltpu.VMEM((3 * slots, lanes), jnp.float32),
            pltpu.VMEM((stage_count, 2, 8, stage_rows), jnp.float32),
            pltpu.VMEM((stage_count, 8, stage_rows), jnp.float32),
            pltpu.VMEM((stage_count, 8, stage_rows), jnp.float32),
            pltpu.VMEM((stage_count, 8, stage_rows), jnp.float32),
            pltpu.VMEM((4, group_rows, width), jnp.bfloat16),
            pltpu.VMEM(centroids.shape, jnp.bfloat16),
            pltpu.VMEM((4, 8, lanes), jnp.float32),
            pltpu.VMEM((3, 8, lanes), jnp.float32),
            pltpu.VMEM((chunk_count, 16, lanes), jnp.float32),
            pltpu.VMEM((clu_count, 16, lanes), jnp.float32),
            dma((3,)),
            dma((clu_count,)),
            dma((clu_count,)),
            dma((clu_count,)),
            dma((clu_count,)),
            dma((clu_count,)),
            dma((clu_count,)),
            dma((2 * chunk_count,)),
            dma((2 * chunk_count,)),
            dma((2 * chunk_count,)),
            dma((2 * chunk_count,)),
            dma((3,)),
            dma((3,)),
            dma((3,)),
            dma((3,)),
            dma((1,)),
            dma((1,)),
            dma((clu_count,)),
            dma((clu_count,)),
        ],
        compiler_params=pltpu.CompilerParams(
            collective_id=0, has_side_effects=True, vmem_limit_bytes=48 * 1024 * 1024
        ),
        name="exchange",
    )(send_units, send_ids, slot, new_unit, centroids)
    return (dup.reshape(rows), best.reshape(new_count))


def solution(mesh):
    return jax.shard_map(
        shards,
        mesh=mesh,
        in_specs=(
            P(("clu", "grp"), None),
            P(("clu", "grp")),
            P(("clu", "grp"), None),
            P(("clu", "grp"), None),
        ),
        out_specs=(P(("clu", "grp")), P(("clu", "grp"))),
        check_vma=False,
    )
```

time: 159 us -> 80.8 us (0.51)
  blocking collectives: 102 us -> 0 us
  Pallas kernels: 0 us -> 74.1 us
  matrix products: 13.9 us -> 0 us
  between operations: 14.1 us -> 0.64 us
  starting transfers between devices: 8.96 us -> 0 us
  other arithmetic: 7.88 us -> 0 us
  waiting for transfers between devices: 3.5 us -> 0 us
  local copies, waits for them, and re-layouts: 8.38 us -> 5.67 us
    pallas_call x0 -> x2, Pallas kernels: none -> 74.1 us  [the longest x1 70.3 us: shards(): pl.pallas_call(functools.partial(exchange_kernel, clu_count, cap, new_cou...]
    all_to_all x1 -> x0, blocking collectives: 44.2 us -> none  [shards(): lax.all_to_all(send_units, 'clu', split_axis=0, concat_axis=0, tiled=True)]
    all_gather x2 -> x0, blocking collectives: 36.5 us -> none  [the longest x1 31.3 us: shards(): lax.all_gather(new_unit, 'clu', axis=0, tiled=True)]
    pmax x1 -> x0, blocking collectives: 21.4 us -> none  [shards(): overall = lax.pmax(partial_best, 'clu')]
    dot_general x3 -> x0, matrix products: 13.9 us -> none  [the longest x2 13.7 us: pair_scores(): lax.dot_general(left_units, right_units, (((1,), (1,)), ((), ())), prefer...]
    all_to_all x2 -> x0, starting transfers between devices: 8.89 us -> none  [the longest x1 5.3 us: shards(): lax.all_to_all(best_match.reshape(clu_count, slot_cap), 'clu', split_axis...]
    unnamed x8 -> x12, local copies, waits for them, and re-layouts: 0.02 us -> 5.67 us
    scatter x1 -> x0, local copies, waits for them, and re-layouts: 3.77 us -> none  [shards(): send_ids = jnp.full((slot_total,), -1.0, jnp.bfloat16).at[row_slot].set(c...]
  transfers between devices with their start and end apart: 4 -> 0, of which waited for: 1 -> 0; matrix products, arithmetic and copies ran while one was open for 13% -> 0% of each run, Pallas kernels for 0% -> 0%
where the time goes in v1:
time: 80.8 us; the launch traced here: 80.4 us
  Pallas kernels  74.1 us (92%)
  local copies, waits for them, and re-layouts  5.67 us (7%)
    pallas_call x1, Pallas kernels, shards(): pl.pallas_call(functools.partial(exchange_kernel, clu_count, cap, new_cou...  70.3 us
    unnamed x12, local copies, waits for them, and re-layouts  5.67 us
    pallas_call x1, Pallas kernels, shards(): pl.pallas_call(functools.partial(pack_kernel, clu_count, cap), out_shape=...  3.77 us

profile of v1, /device:TPU:0, one launch (start us, length us, event | category | flops | bytes accessed | tf_op | source)
XLA Modules:
  0.0 80.4 jit_solution(16680140790325154000)
XLA Ops:
  0.6 3.8 %pack.1 = (bf16[1024,768]{1,0:T(8,128)(2,1)}, f32[8,8,128]{2,1,0:T(8,128)}, s32[1,512]{1,0:T(1,128)}, bf16[16,768]{1,0:T(8,128)(2,1)}) custom-call(bf16[512,768]{1,0:T(8,128)(2,1)} %emb_ref.1, s32[1,512]{1,0:T(1,128)} %bitcast.5, bf16[16,768]{1,0:T(8,128)(2,1)} %new_ref.1), custom_call_target="tpu_custom_call" | custom-call | tf_op jit(solution)/shard_map/pack/pallas_call | solution.py:432
  4.4 0.0 copy-start
  4.4 1.4 %copy-done = bf16[1024,768]{1,0:T(8,128)(2,1)S(1)} copy-done((bf16[1024,768]{1,0:T(8,128)(2,1)S(1)}, bf16[1024,768]{1,0:T(8,128)(2,1)}, u32[]{:S(2)}) %copy-start) | copy-done | bytes 1572888
  5.8 0.0 copy-start.1
  5.8 1.0 %copy-done.1 = bf16[256,768]{1,0:T(8,128)(2,1)S(1)} copy-done((bf16[256,768]{1,0:T(8,128)(2,1)S(1)}, bf16[256,768]{1,0:T(8,128)(2,1)}, u32[]{:S(2)}) %copy-start.1) | copy-done | bytes 393240
  6.8 0.0 copy-start.2
  6.8 0.8 copy-done.2
  7.6 0.0 copy-start.3
  7.6 0.7 copy-done.3
  8.3 0.0 copy-start.4
  8.3 0.7 copy-done.4
  9.0 70.3 %exchange.1 = (f32[1,512]{1,0:T(1,128)S(1)}, f32[1,16]{1,0:T(1,128)S(1)}) custom-call(bf16[1024,768]{1,0:T(8,128)(2,1)S(1)} %copy-done, f32[8,8,128]{2,1,0:T(8,128)S(1)} %copy-done.2, s32[1,512]{1,0:T(1,128)S(1)} %copy-done.4, bf16[16,768]{1,0:T(8,128)(2,1)S(1)} %copy-done.3, bf16[256,768]{1,0:T(8,128)(2,1)S(1)} %copy-done.1), custom_call_target="tpu_custom_call" | custom-call | tf_op jit(solution)/shard_map/exchange/pallas_call | solution.py:447
  79.3 0.6 copy.8
  79.9 0.5 copy.9
Async XLA Ops:
  4.4 1.4 %copy-start = (bf16[1024,768]{1,0:T(8,128)(2,1)S(1)}, bf16[1024,768]{1,0:T(8,128)(2,1)}, u32[]{:S(2)}) copy-start(bf16[1024,768]{1,0:T(8,128)(2,1)} %get-tuple-element.8.send_ref) | copy-start | bytes 4718596
  5.8 1.0 %copy-start.1 = (bf16[256,768]{1,0:T(8,128)(2,1)S(1)}, bf16[256,768]{1,0:T(8,128)(2,1)}, u32[]{:S(2)}) copy-start(bf16[256,768]{1,0:T(8,128)(2,1)} %cent_ref.1) | copy-start | bytes 1179652
  6.8 0.8 copy-start.2
  7.6 0.7 copy-start.3
  8.3 0.7 copy-start.4

commit v2 on v1

--- a/solution.py
+++ b/solution.py
@@ -9,7 +9,7 @@
 
 epsilon = 1e-06
 lanes = 128
-chunk_order = (0, 1, 6, 7, 2, 3, 4, 5)
+chunk_order = (0, 1, 2, 3, 4, 5, 6, 7)
 chunk_count = len(chunk_order)
 stage_count = chunk_count // 2
 MESH = pl.DeviceIdType.MESH
@@ -27,54 +27,23 @@
     )
 
 
-def pack_kernel(clu_count, cap, emb_ref, cluster_ref, new_ref, send_ref, ids_ref, slot_ref, unit_ref):
-    per_chunk = clu_count // chunk_count
-    rows = emb_ref.shape[0]
-    slots = clu_count * cap
-    me = lax.axis_index("clu")
-    unit_ref[...] = normalize(new_ref[...])
-    cluster = cluster_ref[...]
-    distance = (cluster & (clu_count - 1)) ^ me
-    far_chunk = distance // per_chunk
-    place = jnp.zeros_like(distance)
-    for position, chunk in enumerate(chunk_order):
-        place = jnp.where(far_chunk == chunk, position, place)
-    place = place * per_chunk + distance % per_chunk
-    owner_hot = lax.broadcasted_iota(jnp.int32, (clu_count, rows), 0) == place
-    before = lax.broadcasted_iota(jnp.int32, (rows, rows), 0) < lax.broadcasted_iota(
-        jnp.int32, (rows, rows), 1
-    )
-    preceding = jnp.dot(
-        owner_hot.astype(jnp.bfloat16),
-        before.astype(jnp.bfloat16),
-        preferred_element_type=jnp.float32,
-    )
-    rank = jnp.sum(jnp.where(owner_hot, preceding, 0.0), axis=0, keepdims=True).astype(jnp.int32)
-    slot = place * cap + rank
-    slot_ref[...] = slot
-    chosen = (lax.broadcasted_iota(jnp.int32, (slots, rows), 0) == slot).astype(jnp.bfloat16)
-    units = normalize(emb_ref[...])
-    send_ref[...] = jnp.dot(chosen, units, preferred_element_type=jnp.float32).astype(jnp.bfloat16)
-    marks = jnp.broadcast_to((cluster + 1).astype(jnp.float32), (8, rows)).astype(jnp.bfloat16)
-    slot_marks = pair_scores(marks, chosen)
-    lane_block = lax.broadcasted_iota(jnp.int32, (8, lanes), 1) // cap
-    for block in range(clu_count):
-        chunk, inner = divmod(block, per_chunk)
-        tile = slot_marks[:, chunk * lanes : (chunk + 1) * lanes]
-        ids_ref[block] = jnp.where(lane_block == inner, tile, 0.0)
-
-
 def exchange_kernel(
     clu_count,
     cap,
     new_count,
+    emb_hbm,
+    cluster_hbm,
+    new_hbm,
+    cent_hbm,
+    dup_ref,
+    best_ref,
+    emb_ref,
+    cluster_ref,
+    new_ref,
+    cent_ref,
+    units,
     send_ref,
     ids_ref,
-    slot_ref,
-    new_ref,
-    cent_ref,
-    dup_ref,
-    best_ref,
     held,
     held_ids,
     marks,
@@ -146,13 +115,13 @@
         pl.semaphore_signal(barrier, inc=1, device_id=near(step), device_id_type=MESH)
 
     local = [
-        pltpu.make_async_copy(send_ref.at[pl.ds(0, cap)], held.at[block_rows(0)], local_sem.at[0]),
-        pltpu.make_async_copy(ids_ref.at[0], held_ids.at[0, 0], local_sem.at[1]),
-        pltpu.make_async_copy(new_ref, new_held.at[0, pl.ds(0, new_count)], local_sem.at[2]),
+        pltpu.make_async_copy(new_hbm, new_ref, local_sem.at[0]),
+        pltpu.make_async_copy(cluster_hbm, cluster_ref, local_sem.at[1]),
+        pltpu.make_async_copy(emb_hbm, emb_ref, local_sem.at[2]),
+        pltpu.make_async_copy(cent_hbm, cent_ref, local_sem.at[3]),
     ]
     for copy in local:
         copy.start()
-    pl.semaphore_wait(barrier, clu_count - 1 + 3)
 
     new_copies = []
     data_copies = [None]
@@ -160,7 +129,7 @@
     for block in range(1, clu_count):
         new_copies.append(
             remote(
-                new_ref,
+                new_held.at[0, pl.ds(0, new_count)],
                 new_held.at[0, pl.ds(block * new_count, new_count)],
                 new_send.at[block],
                 new_recv.at[block],
@@ -185,15 +154,62 @@
                 far(block),
             )
         )
+
+    local[0].wait()
+    new_held[0, 0:new_count, :] = normalize(new_ref[...])
+    local[1].wait()
+    cluster = cluster_ref[...]
+    rows = cluster.shape[1]
+    distance = (cluster & (clu_count - 1)) ^ me
+    far_chunk = distance // per_chunk
+    place = jnp.zeros_like(distance)
+    for index, chunk in enumerate(chunk_order):
+        place = jnp.where(far_chunk == chunk, index, place)
+    place = place * per_chunk + distance % per_chunk
+    owner_hot = lax.broadcasted_iota(jnp.int32, (clu_count, rows), 0) == place
+    before = lax.broadcasted_iota(jnp.int32, (rows, rows), 0) < lax.broadcasted_iota(
+        jnp.int32, (rows, rows), 1
+    )
+    preceding = jnp.dot(
+        owner_hot.astype(jnp.bfloat16),
+        before.astype(jnp.bfloat16),
+        preferred_element_type=jnp.float32,
+    )
+    rank = jnp.sum(jnp.where(owner_hot, preceding, 0.0), axis=0, keepdims=True).astype(jnp.int32)
+    slot = place * cap + rank
+    id_values = jnp.broadcast_to((cluster + 1).astype(jnp.float32), (8, rows)).astype(jnp.bfloat16)
+    chunk_slot = lax.broadcasted_iota(jnp.int32, (lanes, rows), 0)
+    inner_block = lax.broadcasted_iota(jnp.int32, (8, lanes), 1) // cap
+    local[2].wait()
+    units[...] = normalize(emb_ref[...])
+    pl.semaphore_wait(barrier, clu_count - 1 + 3)
     for copy in new_copies:
         copy.start()
-    for block in range(1, clu_count):
-        id_copies[block].start()
-        data_copies[block].start()
-
-    own_acc[...] = jnp.full(own_acc.shape, -1.0, jnp.float32)
-    mate_acc[...] = jnp.full(mate_acc.shape, -1.0, jnp.float32)
-    cent_unit[...] = normalize(cent_ref[...])
+
+    def pack(chunk):
+        chosen = (chunk_slot + chunk * lanes == slot).astype(jnp.bfloat16)
+        packed = jnp.dot(chosen, units[...], preferred_element_type=jnp.float32).astype(
+            jnp.bfloat16
+        )
+        tile = pair_scores(id_values, chosen)
+        for inner in range(per_chunk):
+            block = chunk * per_chunk + inner
+            if per_chunk == 1:
+                own_tile = tile
+            else:
+                own_tile = jnp.where(inner_block == inner, tile, 0.0)
+            if block == 0:
+                held_ids[0, 0] = own_tile
+                held[block_rows(0), :] = packed[0:cap]
+            else:
+                ids_ref[block] = own_tile
+        if per_chunk > 1 or chunk > 0:
+            send_ref[chunk * lanes : (chunk + 1) * lanes, :] = packed
+
+    def dispatch(chunk):
+        for block in range(max(1, chunk * per_chunk), (chunk + 1) * per_chunk):
+            id_copies[block].start()
+            data_copies[block].start()
 
     forwards = {}
 
@@ -210,10 +226,7 @@
     def pass_on(chunk):
         for inner in range(per_chunk):
             block = chunk * per_chunk + inner
-            if block == 0:
-                local[0].wait()
-                local[1].wait()
-            else:
+            if block > 0:
                 id_copies[block].wait_recv()
                 data_copies[block].wait_recv()
         src_rows = pl.ds(chunk_row(chunk, 0), half)
@@ -250,6 +263,30 @@
         kept = jnp.where(matched, scores, -1.0)
         return jnp.max(kept.reshape(stage_rows // 8, 8, stage_rows), axis=0)
 
+    def tile_rows(stage, kind):
+        start = stage * (3 * stage_rows) + kind * stage_rows
+        if not isinstance(start, int):
+            start = pl.multiple_of(start, stage_rows)
+        return pl.ds(start, stage_rows)
+
+    def own_pair(kind, left, right):
+        rows = tile_rows(left, kind)
+        mark = marks[rows, :]
+        matched = jnp.concatenate([mark, mark], axis=1) == id_rows[right, 0][0:1]
+        if kind == 0:
+            row_id = lax.broadcasted_iota(jnp.int32, (stage_rows, stage_rows), 0)
+            col_id = lax.broadcasted_iota(jnp.int32, (stage_rows, stage_rows), 1)
+            matched = matched & (row_id - col_id != (right - left) * stage_rows)
+        scores = pair_scores(held[rows, :], held[tile_rows(right, 0), :])
+        own_acc[right] = jnp.maximum(own_acc[right], fold(scores, matched))
+
+    def mate_pair(left, right):
+        rows = tile_rows(left, 2)
+        mark = marks[rows, :]
+        matched = jnp.concatenate([mark, mark], axis=1) == id_rows[right, 1][0:1]
+        scores = pair_scores(held[rows, :], held[tile_rows(right, 1), :])
+        mate_acc[right] = jnp.maximum(mate_acc[right], fold(scores, matched))
+
     def compute(stage):
         receive(2 * stage)
         receive(2 * stage + 1)
@@ -257,38 +294,41 @@
         def body(step, carry):
             left = jnp.minimum(step, stage)
             right = jnp.where(step <= stage, stage, step - stage - 1)
-            left_base = left * (3 * stage_rows)
-            right_base = right * (3 * stage_rows)
-            own_cols = held[pl.ds(pl.multiple_of(right_base, stage_rows), stage_rows), :]
-            mate_cols = held[
-                pl.ds(pl.multiple_of(right_base + stage_rows, stage_rows), stage_rows), :
-            ]
-            own_ids = id_rows[right, 0][0:1]
-            mate_ids = id_rows[right, 1][0:1]
-            best = own_acc[right]
             for kind in range(3):
-                rows = pl.ds(
-                    pl.multiple_of(left_base + kind * stage_rows, stage_rows), stage_rows
-                )
-                others = held[rows, :]
-                mark = marks[rows, :]
-                mark = jnp.concatenate([mark, mark], axis=1)
-                matched = mark == own_ids
-                if kind == 0:
-                    row_id = lax.broadcasted_iota(jnp.int32, (stage_rows, stage_rows), 0)
-                    col_id = lax.broadcasted_iota(jnp.int32, (stage_rows, stage_rows), 1)
-                    shift = (right - left) * stage_rows
-                    matched = matched & (row_id - col_id != shift)
-                best = jnp.maximum(best, fold(pair_scores(others, own_cols), matched))
-                if kind == 2:
-                    mate_acc[right] = jnp.maximum(
-                        mate_acc[right],
-                        fold(pair_scores(others, mate_cols), mark == mate_ids),
-                    )
-            own_acc[right] = best
+                own_pair(kind, left, right)
+            mate_pair(left, right)
             return carry
 
         lax.fori_loop(0, 2 * stage + 1, body, 0)
+
+    def compute_last():
+        last = stage_count - 1
+
+        def own_rows(step, carry):
+            own_pair(0, last, step)
+            return carry
+
+        def own_cols(step, carry):
+            for kind in range(3):
+                own_pair(kind, step, last)
+            return carry
+
+        def other_rows(step, carry):
+            own_pair(1, last, step)
+            own_pair(2, last, step)
+            mate_pair(last, step)
+            return carry
+
+        def mate_cols(step, carry):
+            mate_pair(step, last)
+            return carry
+
+        lax.fori_loop(0, stage_count, own_rows, 0)
+        lax.fori_loop(0, last, own_cols, 0)
+        receive(2 * last)
+        receive(2 * last + 1)
+        lax.fori_loop(0, last, mate_cols, 0)
+        lax.fori_loop(0, stage_count, other_rows, 0)
 
     group_rows = clu_count * new_count
     cross_new = remote(
@@ -308,7 +348,6 @@
     ]
 
     def new_first():
-        local[2].wait()
         for copy in new_copies:
             copy.wait_recv()
         cross_new.start()
@@ -335,21 +374,34 @@
         for copy in part_copies:
             copy.start()
 
+    pack(0)
+    for chunk in range(1, chunk_count):
+        pack(chunk)
+        if chunk == 1:
+            if per_chunk > 1:
+                dispatch(0)
+        else:
+            dispatch(chunk - 1)
+    own_acc[...] = jnp.full(own_acc.shape, -1.0, jnp.float32)
+    mate_acc[...] = jnp.full(mate_acc.shape, -1.0, jnp.float32)
+    dispatch(chunk_count - 1)
     pass_on(0)
+    local[3].wait()
+    cent_unit[...] = normalize(cent_ref[...])
     pass_on(1)
     new_first()
     pass_on(2)
+    pass_on(3)
     new_second()
-    pass_on(3)
-    new_third()
     compute(0)
     pass_on(4)
+    new_third()
     pass_on(5)
     compute(1)
     pass_on(6)
+    compute(2)
     pass_on(7)
-    compute(2)
-    compute(3)
+    compute_last()
 
     mate_copy = remote(mate_acc, mate_in, mate_send.at[0], mate_recv.at[0], near(1))
     mate_copy.start()
@@ -391,7 +443,6 @@
     for copy in messages:
         copy.wait()
 
-    slot = slot_ref[...]
     lane_block = lax.broadcasted_iota(jnp.int32, (1, lanes), 1) // cap
     row_list = []
     for chunk in range(chunk_count):
@@ -429,18 +480,6 @@
     assert lax.axis_size("grp") == 4
     vmem = pl.BlockSpec(memory_space=pltpu.VMEM)
     anywhere = pl.BlockSpec(memory_space=pl.ANY)
-    send_units, send_ids, slot, new_unit = pl.pallas_call(
-        functools.partial(pack_kernel, clu_count, cap),
-        out_shape=(
-            jax.ShapeDtypeStruct((slots, width), jnp.bfloat16),
-            jax.ShapeDtypeStruct((clu_count, 8, lanes), jnp.float32),
-            jax.ShapeDtypeStruct((1, rows), jnp.int32),
-            jax.ShapeDtypeStruct((new_count, width), jnp.bfloat16),
-        ),
-        in_specs=[vmem] * 3,
-        out_specs=(vmem,) * 4,
-        name="pack",
-    )(embeddings, cluster_of.reshape(1, rows), new_rows)
     dma = pltpu.SemaphoreType.DMA
     group_rows = clu_count * new_count
     stage_rows = 2 * lanes
@@ -450,9 +489,16 @@
             jax.ShapeDtypeStruct((1, rows), jnp.float32),
             jax.ShapeDtypeStruct((1, new_count), jnp.float32),
         ),
-        in_specs=[anywhere, anywhere, vmem, anywhere, vmem],
+        in_specs=[anywhere] * 4,
         out_specs=(vmem, vmem),
         scratch_shapes=[
+            pltpu.VMEM((rows, width), jnp.bfloat16),
+            pltpu.VMEM((1, rows), jnp.int32),
+            pltpu.VMEM((new_count, width), jnp.bfloat16),
+            pltpu.VMEM(centroids.shape, jnp.bfloat16),
+            pltpu.VMEM((rows, width), jnp.bfloat16),
+            pltpu.VMEM((slots, width), jnp.bfloat16),
+            pltpu.VMEM((clu_count, 8, lanes), jnp.float32),
             pltpu.VMEM((3 * slots, width), jnp.bfloat16),
             pltpu.VMEM((3, clu_count, 8, lanes), jnp.float32),
             pltpu.VMEM((3 * slots, lanes), jnp.float32),
@@ -466,7 +512,7 @@
             pltpu.VMEM((3, 8, lanes), jnp.float32),
             pltpu.VMEM((chunk_count, 16, lanes), jnp.float32),
             pltpu.VMEM((clu_count, 16, lanes), jnp.float32),
-            dma((3,)),
+            dma((4,)),
             dma((clu_count,)),
             dma((clu_count,)),
             dma((clu_count,)),
@@ -487,10 +533,10 @@
             dma((clu_count,)),
         ],
         compiler_params=pltpu.CompilerParams(
-            collective_id=0, has_side_effects=True, vmem_limit_bytes=48 * 1024 * 1024
+            collective_id=0, has_side_effects=True, vmem_limit_bytes=67043328
         ),
         name="exchange",
-    )(send_units, send_ids, slot, new_unit, centroids)
+    )(embeddings, cluster_of.reshape(1, rows), new_rows, centroids)
     return (dup.reshape(rows), best.reshape(new_count))
 
 

time: 80.8 us -> 64.5 us (0.80)
  Pallas kernels: 74.1 us -> 61.9 us
  local copies, waits for them, and re-layouts: 5.67 us -> 1.8 us
    pallas_call x1, Pallas kernels: 70.3 us -> 61.9 us  [shards(): pl.pallas_call(functools.partial(exchange_kernel, clu_count, cap, new_cou...]
    unnamed x12 -> x6, local copies, waits for them, and re-layouts: 5.67 us -> 1.8 us
    pallas_call x1 -> x0, Pallas kernels: 3.77 us -> none  [shards(): pl.pallas_call(functools.partial(pack_kernel, clu_count, cap), out_shape=...]
where the time goes in v2:
time: 64.5 us; the launch traced here: 64.3 us
  Pallas kernels  61.9 us (96%)
  local copies, waits for them, and re-layouts  1.8 us (3%)
  between operations  0.65 us (1%)
    pallas_call x1, Pallas kernels, shards(): pl.pallas_call(functools.partial(exchange_kernel, clu_count, cap, new_cou...  61.9 us
    unnamed x6, local copies, waits for them, and re-layouts  1.8 us

profile of v2, /device:TPU:0, one launch (start us, length us, event | category | flops | bytes accessed | tf_op | source)
XLA Modules:
  0.0 64.3 jit_solution(1197663055775004156)
XLA Ops:
  0.6 61.9 %exchange.1 = (f32[1,512]{1,0:T(1,128)}, f32[1,16]{1,0:T(1,128)}) custom-call(bf16[512,768]{1,0:T(8,128)(2,1)} %emb_hbm.1, s32[1,512]{1,0:T(1,128)} %bitcast.3, bf16[16,768]{1,0:T(8,128)(2,1)} %new_hbm.1, bf16[256,768]{1,0:T(8,128)(2,1)} %cent_hbm.1), custom_call_target="tpu_custom_call" | custom-call | tf_op jit(solution)/shard_map/exchange/pallas_call | solution.py:486
  62.5 0.0 copy-start
  62.5 0.7 %copy-done = f32[1,512]{1,0:T(1,128)S(1)} copy-done((f32[1,512]{1,0:T(1,128)S(1)}, f32[1,512]{1,0:T(1,128)}, u32[]{:S(2)}) %copy-start) | copy-done | bytes 2072
  63.2 0.0 copy-start.1
  63.2 0.6 copy.8
  63.8 0.1 copy-done.1
  63.8 0.5 copy.9
Async XLA Ops:
  62.5 0.7 %copy-start = (f32[1,512]{1,0:T(1,128)S(1)}, f32[1,512]{1,0:T(1,128)}, u32[]{:S(2)}) copy-start(f32[1,512]{1,0:T(1,128)} %get-tuple-element.4) | copy-start | bytes 6148
  63.2 0.6 copy-start.1
